TPU v7x, 32 devices: a whole 2x2x4 slice. The times are simulated.
32 devices in a mesh: slab: 4 (over x, core), row: 8 (over z, y).
Axes of the slice: x: 2, y: 2, z: 4, core: 2. Of those that a mesh axis runs over, the one named last changes fastest.
Arguments:
- rhs: bfloat16 [3, 2, 64, 8192], P(None, None, None, 'row'), may hold values from -6 to 6
- operator: bfloat16 [4, 2, 8192, 8192], P('slab', None, 'row'), may hold values from -0.046875 to 0.046875
- sources: bfloat16 [4, 3, 2, 64, 8192], P('slab', None, None, None, 'row'), may hold values from -6 to 6
- skeleton: int32 [4, 8192], P('slab'), may hold values from 0 to 8191, each once within a row
Outputs:
- outgoing: bfloat16 [4, 3, 2, 64, 8192], P('slab', None, None, None, 'row')
Inputs may be any that keep to these rules, and one draw needn't show every extreme that they name: Each row of skeleton is a permutation of 0 to 8191.
All inputs are finite; a program needn't handle non-finite values.
Results may differ from a plain program's by a relative error of at most 0.0055.
Values may be sent and summed in bfloat16 or wider, within the bound.
A program may use at most 192 MiB of HBM per device.

v0:
```python
import jax
import jax.numpy as jnp
from jax import lax
from jax.sharding import PartitionSpec as P


def passed_along(value, axis, steps):
    count = lax.axis_size(axis)
    leading, last = (max(0, -steps), min(count, count - steps))
    return lax.ppermute(value, axis, [(source, source + steps) for source in range(leading, last)])


def complex_apply(inputs, matrix):
    count = inputs.shape[0]
    width = inputs.shape[2]
    depth = inputs.shape[3]
    rows = matrix.shape[1]
    flat = inputs.reshape(count * 2 * width, depth)
    mflat = matrix.reshape(2 * rows, depth)
    joined = lax.dot_general(
        flat, mflat, (((1,), (1,)), ((), ())), preferred_element_type=jnp.float32
    )
    joined = joined.reshape(count, 2, width, 2, rows)
    real_part = joined[:, 0, :, 0] - joined[:, 1, :, 1]
    imag_part = joined[:, 1, :, 0] + joined[:, 0, :, 1]
    return jnp.stack([real_part, imag_part], axis=1)


def permute_columns(matrix, order):
    total_cols = matrix.shape[2]
    inverse = (
        jnp.zeros((total_cols,), jnp.int32).at[order].set(jnp.arange(total_cols, dtype=jnp.int32))
    )
    return jnp.take(matrix, inverse, axis=2)


def on_device(rhs, operator, sources, skeleton):
    matrix = operator[0]
    order = skeleton[0]
    permuted = permute_columns(matrix, order)
    slab_index = lax.axis_index("slab")
    sections = lax.axis_size("slab")
    local_sources = sources[0]
    result = jnp.zeros(local_sources.shape, jnp.bfloat16)
    incoming = rhs
    for section in range(sections):
        value = (
            complex_apply(lax.all_gather(incoming, "row", axis=3, tiled=True), permuted)
            + local_sources.astype(jnp.float32)
        ).astype(jnp.bfloat16)
        result = jnp.where(slab_index == section, value, result)
        if section + 1 < sections:
            received = passed_along(value, "slab", 1)
            incoming = jnp.where(slab_index == 0, rhs, received)
    return result[None]


def solution(mesh):
    return jax.shard_map(
        on_device,
        mesh=mesh,
        in_specs=(
            P(None, None, None, "row"),
            P("slab", None, "row", None),
            P("slab", None, None, None, "row"),
            P("slab", None),
        ),
        out_specs=P("slab", None, None, None, "row"),
        check_vma=False,
    )
```

profile of v0, /device:TPU:3, one launch (start us, length us, event | category | flops | bytes accessed | tf_op | source)
XLA Modules:
  0.0 894.7 jit_solution(5125702711377993225)
XLA Ops:
  7.3 82.2 %copy.27 = bf16[1,2,1024,8192]{2,1,3,0:T(2,128)(2,1)} copy(bf16[1,2,1024,8192]{3,2,1,0:T(8,128)(2,1)} %param.5) | data formatting | bytes 67108864 | tf_op args[1]
  89.6 30.5 %scatter_custom_fusion = s32[8192]{0:T(1024)S(1)} fusion(s32[8192]{0:T(1024)S(1)} %bitcast.77, s32[8192]{0:T(1024)S(1)} %iota.3, s32[]{:T(128)} %constant.11.clone.1), kind=kCustom, calls=%fused_computation.58 | custom fusion | bytes 32772 | tf_op jit(solution)/shard_map/scatter | solution.py:32
  120.1 193.6 %gather_fusion = bf16[8192,2,1024]{2,1,0:T(2,128)(2,1)} fusion(bf16[2,1024,8192]{1,0,2:T(2,128)(2,1)} %bitcast.74, s32[8192]{0:T(1024)S(1)} %fusion.27), kind=kCustom, calls=%fused_computation | custom fusion | bytes 67141632 | tf_op jit(solution)/shard_map/jit(_take)/gather | solution.py:34
  313.7 50.2 %broadcast_select_fusion = bf16[8192,2,1024]{2,1,0:T(2,128)(2,1)} fusion(bf16[8192,2,1024]{2,1,0:T(2,128)(2,1)} %gather_fusion, pred[8192]{0:T(1024)(128)(4,1)S(1)} %compare_and_fusion), kind=kLoop, calls=%fused_computation.2 | loop fusion | flops 16777216 | bytes 67117056 | tf_op jit(solution)/shard_map/jit(_take)/select_n | solution.py:34
  363.9 23.3 %copy.75 = bf16[1024,8,2,1024]{3,1,2,0:T(8,128)(2,1)} copy(bf16[1024,8,2,1024]{3,2,1,0:T(2,128)(2,1)} %bitcast.75) | data formatting | bytes 67108864
  387.2 22.2 %convolution_bitcast_fusion = f32[384,2048]{0,1:T(8,128)S(1)} fusion(bf16[2048,8192]{0,1:T(8,128)(2,1)} %bitcast.76, bf16[384,8192]{1,0:T(8,128)(2,1)} %bitcast.78), kind=kOutput, calls=%fused_computation.9 | convolution fusion | flops 12884901888 | bytes 42991616 | tf_op jit(solution)/shard_map/dot_general | solution.py:20
  409.3 5.3 reshape.357
  414.6 9.5 %fusion.30 = (f32[3,1,64,1,1024]{2,1,0,4,3:T(1,128)}, f32[3,1,64,1,1024]{2,1,0,4,3:T(1,128)S(1)}, f32[3,1,64,1,1024]{2,1,0,4,3:T(1,128)}, f32[3,1,64,1,1024]{2,1,0,4,3:T(1,128)S(1)}) fusion(f32[3,2,64,2,1024]{2,1,0,4,3:T(2,128)} %reshape.357), kind=kLoop, calls=%fused_computation.60 | loop fusion | bytes 6291456 | tf_op jit(solution)/shard_map/slice | solution.py:24
  424.2 4.6 copy.71
  428.8 4.6 copy.72
  433.4 3.2 copy.73
  436.6 3.3 copy.74
  444.5 3.3 collective-permute-done
  450.0 50.2 %fusion.36 = bf16[2,1024,8192,1,1]{1,0,2,4,3:T(2,128)(2,1)} fusion(bf16[8192,2,1024]{2,1,0:T(2,128)(2,1)} %gather_fusion, pred[8192]{0:T(1024)(128)(4,1)S(1)} %compare_and_fusion), kind=kLoop, calls=%fused_computation.61 | loop fusion | flops 16777216 | bytes 67117056 | tf_op jit(solution)/shard_map/jit(_take)/select_n | solution.py:34
  500.2 81.0 %copy.55 = bf16[2,1024,8192,1,1]{2,1,3,0,4:T(8,128)(2,1)} copy(bf16[2,1024,8192,1,1]{1,0,2,4,3:T(2,128)(2,1)} %fusion.36) | data formatting | bytes 67108864 | tf_op jit(solution)/shard_map/jit(_take)/select_n | solution.py:34
  581.2 20.6 %fusion.4 = f32[3,2,64,2,1024]{4,2,0,3,1:T(8,128)} fusion(bf16[2,1024,8192,1,1]{2,1,3,0,4:T(8,128)(2,1)} %copy.55, bf16[3,2,64,8192]{3,2,1,0:T(8,128)(2,1)} %all-gather.7.cloned.1.call-done), kind=kOutput, calls=%fused_computation.7 | convolution fusion | flops 12884901888 | bytes 42991616 | tf_op jit(solution)/shard_map/dot_general | solution.py:20
  601.8 3.3 fusion.20
  606.7 11.9 %collective-permute-done.1 = bf16[3,2,64,1024]{3,2,1,0:T(8,128)(2,1)S(1)} collective-permute-done((bf16[3,2,64,1024]{3,2,1,0:T(8,128)(2,1)S(1)}, bf16[3,2,64,1024]{3,2,1,0:T(8,128)(2,1)S(1)}, u32[]{:S(2)}, u32[]{:S(2)}) %collective-permute-start.1) | collective-permute-done | bytes 786464 | tf_op jit(solution)/shard_map/ppermute | solution.py:10
  619.6 107.7 %all-gather.9.cloned.1.call-done = bf16[3,2,64,8192]{3,2,1,0:T(8,128)(2,1)} async-done(((bf16[3,2,64,1024]{3,2,1,0:T(8,128)(2,1)}), bf16[3,2,64,8192]{3,2,1,0:T(8,128)(2,1)}) %all-gather.9.cloned.1.call-update) | async-done | bytes 6291472 | tf_op jit(solution)/shard_map/all_gather | solution.py:48
  727.3 20.7 %fusion.2 = f32[3,2,64,2,1024]{4,2,0,3,1:T(8,128)} fusion(bf16[2,1024,8192,1,1]{2,1,3,0,4:T(8,128)(2,1)} %copy.55, bf16[3,2,64,8192]{3,2,1,0:T(8,128)(2,1)} %all-gather.9.cloned.1.call-done), kind=kOutput, calls=%fused_computation.5 | convolution fusion | flops 12884901888 | bytes 42991616 | tf_op jit(solution)/shard_map/dot_general | solution.py:20
  747.9 3.3 fusion.24
  752.9 4.4 collective-permute-done.2
  758.3 104.6 %all-gather.11.cloned.1.call-done = bf16[3,2,64,8192]{3,2,1,0:T(8,128)(2,1)} async-done(((bf16[3,2,64,1024]{3,2,1,0:T(8,128)(2,1)}), bf16[3,2,64,8192]{3,2,1,0:T(8,128)(2,1)}) %all-gather.11.cloned.1.call-update) | async-done | bytes 6291472 | tf_op jit(solution)/shard_map/all_gather | solution.py:48
  862.9 20.7 %fusion = f32[3,2,64,2,1024]{4,2,0,3,1:T(8,128)} fusion(bf16[2,1024,8192,1,1]{2,1,3,0,4:T(8,128)(2,1)} %copy.55, bf16[3,2,64,8192]{3,2,1,0:T(8,128)(2,1)} %all-gather.11.cloned.1.call-done), kind=kOutput, calls=%fused_computation.3 | convolution fusion | flops 12884901888 | bytes 42991616 | tf_op jit(solution)/shard_map/dot_general | solution.py:20
  (41 shorter events, 17.3 us)
Async XLA Ops:
  6.5 380.6 %all-gather.5.cloned.1.call-start = ((), (), s32[]{:S(2)}) async-start(), calls=%async_computation | async-start | bytes 7077888 | tf_op jit(solution)/shard_map/all_gather | solution.py:48
  7.3 82.3 %copy-start.6 = (s32[1,8192]{1,0:T(1,128)S(1)}, s32[1,8192]{1,0:T(1,128)}, u32[]{:S(2)}) copy-start(s32[1,8192]{1,0:T(1,128)} %param.7) | copy-start | bytes 98308
  7.3 573.9 %all-gather.7.cloned.1.call-start = ((), (), s32[]{:S(2)}) async-start(), calls=%async_computation.1 | async-start | bytes 7077888 | tf_op jit(solution)/shard_map/all_gather | solution.py:48
  439.8 2.2 copy-start.1
  442.0 5.8 copy-start
  443.2 4.6 collective-permute-start
  449.9 277.4 %all-gather.9.cloned.1.call-start = ((), (), s32[]{:S(2)}) async-start(), calls=%async_computation.2 | async-start | bytes 7077888 | tf_op jit(solution)/shard_map/all_gather | solution.py:48
  605.4 13.2 %collective-permute-start.1 = (bf16[3,2,64,1024]{3,2,1,0:T(8,128)(2,1)S(1)}, bf16[3,2,64,1024]{3,2,1,0:T(8,128)(2,1)S(1)}, u32[]{:S(2)}, u32[]{:S(2)}) collective-permute-start(bf16[3,2,64,1024]{3,2,1,0:T(8,128)(2,1)S(1)} %fusion.6), channel_id=1, source_target_pairs={{0,8},{8,16},{16,24},{1,9},{9,17},{17,25},{2,10},{10,18},{18,26},{... | collective-permute-start | bytes 2359304 | tf_op jit(solution)/shard_map/ppermute | solution.py:10
  619.6 243.3 %all-gather.11.cloned.1.call-start = ((), (), s32[]{:S(2)}) async-start(), calls=%async_computation.3 | async-start | bytes 7077888 | tf_op jit(solution)/shard_map/all_gather | solution.py:48
  751.6 5.7 collective-permute-start.2
  883.6 2.3 copy-start.2
  883.6 2.3 copy-start.3
  883.6 2.5 copy-start.4
  883.6 2.8 copy-start.5
Sparse Core Ops, SparseCore 0:
  9.5 98.5 all-gather.4
  450.0 107.4 all-gather.6
  619.7 107.5 all-gather.8
  758.4 104.4 all-gather.10
where the time goes:
time: 905 us; the launch traced here: 895 us
  local copies, waits for them, and re-layouts  443 us (49%)
  waiting for transfers between devices  233 us (26%)
  other arithmetic  118 us (13%)
  matrix products  84.1 us (9%)
  between operations  13.3 us (1%)
    all_gather x4, waiting for transfers between devices, on_device(): lax.all_gather(incoming, 'row', axis=3, tiled=True)  212 us
    gather x1, local copies, waits for them, and re-layouts, permute_columns(): return jnp.take(matrix, inverse, axis=2)  194 us
    unnamed x20, local copies, waits for them, and re-layouts  122 us
    select_n x2, other arithmetic, permute_columns(): return jnp.take(matrix, inverse, axis=2)  100 us
    dot_general x4, matrix products, complex_apply(): lax.dot_general(flat, mflat, (((1,), (1,)), ((), ())), preferred_element_...  84.1 us
    select_n x1, local copies, waits for them, and re-layouts, permute_columns(): return jnp.take(matrix, inverse, axis=2)  81 us
    scatter x1, local copies, waits for them, and re-layouts, permute_columns(): jnp.zeros((total_cols,), jnp.int32).at[order]  30.5 us
    ppermute x3, waiting for transfers between devices, passed_along(): lax.ppermute(value, axis, [(source, source + steps) for source in range(l...  19.5 us
  transfers between devices with their start and end apart: 7, of which 5 were waited for; matrix products, arithmetic and copies ran while one was open for 57% of the time, Pallas kernels for 0%

commit v1 on v0

v1 whole, which is shorter than its diff:
```python
import functools

import jax
import jax.numpy as jnp
from jax import lax
from jax.experimental import pallas as pl
from jax.experimental.pallas import tpu as pltpu
from jax.sharding import PartitionSpec as P

MESH = pl.DeviceIdType.MESH


def ring_to_row(position, count):
    return jnp.where(position < count // 2, 2 * position, 2 * (count - 1 - position) + 1)


def row_to_ring(row, count):
    return jnp.where(row % 2 == 0, row // 2, count - 1 - row // 2)


def kernel(
    slabs, count,
    skel, rhs, op, src, out,
    matrix, recv, xf, xg, xb, acc,
    msem, lsem, right_send, right_recv, left_send, left_recv, pass_send, pass_recv,
):
    batches = rhs.shape[0]
    rows = rhs.shape[1]
    width = rhs.shape[2]
    depth = rows * count
    half = width // 2
    slab = lax.axis_index("slab")
    row = lax.axis_index("row")
    place = row_to_ring(row, count)
    right = ring_to_row((place + 1) % count, count)
    left = ring_to_row((place + count - 1) % count, count)
    first = slab == 0
    inner = slab < slabs - 1

    loads = [
        pltpu.make_async_copy(op.at[pl.ds(part * rows, rows)], matrix.at[pl.ds(part * rows, rows)], msem.at[part])
        for part in range(2)
    ]

    barrier = pltpu.get_barrier_semaphore()
    pl.semaphore_signal(barrier, inc=1, device_id={"slab": slab, "row": right}, device_id_type=MESH)
    pl.semaphore_signal(barrier, inc=1, device_id={"slab": slab, "row": left}, device_id_type=MESH)

    @pl.when(inner)
    def _():
        pl.semaphore_signal(barrier, inc=1, device_id={"slab": slab + 1, "row": row}, device_id_type=MESH)

    @pl.when(jnp.logical_not(first))
    def _():
        pl.semaphore_signal(barrier, inc=1, device_id={"slab": slab - 1, "row": row}, device_id_type=MESH)

    for copy in loads:
        copy.start()
    pl.semaphore_wait(barrier, 2 + jnp.where(inner, 1, 0) + jnp.where(first, 0, 1))

    def block(owner):
        return pl.ds(pl.multiple_of(owner * rows, rows), rows)

    def rightward(batch, step):
        owner = ring_to_row((place + count - step) % count, count)
        piece = recv.at[batch, block(owner)]
        return pltpu.make_async_remote_copy(
            src_ref=piece, dst_ref=piece,
            send_sem=right_send.at[batch, step], recv_sem=right_recv.at[batch, step],
            device_id={"slab": slab, "row": right}, device_id_type=MESH,
        )

    def leftward(batch, step):
        owner = ring_to_row((place + step) % count, count)
        piece = recv.at[batch, block(owner)]
        return pltpu.make_async_remote_copy(
            src_ref=piece, dst_ref=piece,
            send_sem=left_send.at[batch, step], recv_sem=left_recv.at[batch, step],
            device_id={"slab": slab, "row": left}, device_id_type=MESH,
        )

    right_steps = count // 2
    left_steps = count - 1 - right_steps

    def passing(batch):
        return pltpu.make_async_remote_copy(
            src_ref=out.at[batch], dst_ref=recv.at[batch, block(row)],
            send_sem=pass_send.at[batch], recv_sem=pass_recv.at[batch],
            device_id={"slab": jnp.minimum(slab + 1, slabs - 1), "row": row}, device_id_type=MESH,
        )

    def own(batch):
        return pltpu.make_async_copy(rhs.at[batch], recv.at[batch, block(row)], lsem.at[batch])

    def advance(batch, step):
        if step == 0:
            @pl.when(first)
            def _():
                own(batch).start()
                own(batch).wait()

            @pl.when(jnp.logical_not(first))
            def _():
                passing(batch).wait_recv()
        else:
            if step - 1 < right_steps:
                rightward(batch, step - 1).wait_recv()
            if step - 1 < left_steps:
                leftward(batch, step - 1).wait_recv()
        if step < right_steps:
            rightward(batch, step).start()
        if step < left_steps:
            leftward(batch, step).start()

    steps = right_steps + 1
    parts = 8
    span = depth // parts
    unroll = 64
    done = 0

    for batch in range(batches):
        for step in range(done, steps):
            advance(batch, step)

        @pl.loop(0, parts)
        def _(part):
            at = pl.ds(pl.multiple_of(part * span, span), span)
            xf[at, :] = recv[batch, at, :].astype(jnp.float32)

        acc[...] = jnp.zeros_like(acc)
        if batch == 0:
            for copy in loads:
                copy.wait()

        def piece(part):
            base = part * span

            @pl.loop(0, span // unroll)
            def _(chunk):
                for inner_row in range(unroll):
                    index = chunk * unroll + inner_row
                    xg[pl.ds(index, 1), :] = xf[pl.ds(skel[base + index], 1), :]

            xb[...] = xg[...].astype(jnp.bfloat16)
            acc[...] += jnp.dot(
                matrix[:, pl.ds(pl.multiple_of(base, span), span)], xb[...],
                preferred_element_type=jnp.float32,
            )

        @pl.loop(0, parts)
        def _(part):
            piece(part)

        lane = lax.broadcasted_iota(jnp.int32, (rows, width), 1)
        turned = pltpu.roll(acc[rows:, :], half, axis=1)
        total = acc[:rows, :] + jnp.where(lane < half, -turned, turned)
        out[batch] = (total + src[batch].astype(jnp.float32)).astype(jnp.bfloat16)

        @pl.when(inner)
        def _():
            passing(batch).start()

    for batch in range(batches):
        for step in range(right_steps):
            rightward(batch, step).wait_send()
        for step in range(left_steps):
            leftward(batch, step).wait_send()

        @pl.when(inner)
        def _():
            passing(batch).wait_send()


def on_device(rhs, operator, sources, skeleton):
    slabs = lax.axis_size("slab")
    count = lax.axis_size("row")
    batches, two, lanes, rows = rhs.shape
    depth = operator.shape[3]
    width = two * lanes
    flipped = rhs.reshape(batches, width, rows).transpose(0, 2, 1)
    added = sources[0].reshape(batches, width, rows).transpose(0, 2, 1)
    half = max(1, count // 2)
    result = pl.pallas_call(
        functools.partial(kernel, slabs, count),
        out_shape=jax.ShapeDtypeStruct((batches, rows, width), jnp.bfloat16),
        in_specs=[
            pl.BlockSpec(memory_space=pltpu.SMEM),
            pl.BlockSpec(memory_space=pltpu.VMEM),
            pl.BlockSpec(memory_space=pl.ANY),
            pl.BlockSpec(memory_space=pltpu.VMEM),
        ],
        out_specs=pl.BlockSpec(memory_space=pltpu.VMEM),
        scratch_shapes=[
            pltpu.VMEM((2 * rows, depth), jnp.bfloat16),
            pltpu.VMEM((batches, depth, width), jnp.bfloat16),
            pltpu.VMEM((depth, width), jnp.float32),
            pltpu.VMEM((depth // 8, width), jnp.float32),
            pltpu.VMEM((depth // 8, width), jnp.bfloat16),
            pltpu.VMEM((2 * rows, width), jnp.float32),
            pltpu.SemaphoreType.DMA((2,)),
            pltpu.SemaphoreType.DMA((batches,)),
            pltpu.SemaphoreType.DMA((batches, half)),
            pltpu.SemaphoreType.DMA((batches, half)),
            pltpu.SemaphoreType.DMA((batches, half)),
            pltpu.SemaphoreType.DMA((batches, half)),
            pltpu.SemaphoreType.DMA((batches,)),
            pltpu.SemaphoreType.DMA((batches,)),
        ],
        compiler_params=pltpu.CompilerParams(
            collective_id=0, has_side_effects=True, vmem_limit_bytes=60 * 1024 * 1024
        ),
    )(skeleton[0], flipped, operator[0].reshape(2 * rows, depth), added)
    return result.transpose(0, 2, 1).reshape(batches, two, lanes, rows)[None]


def solution(mesh):
    return jax.shard_map(
        on_device,
        mesh=mesh,
        in_specs=(
            P(None, None, None, "row"),
            P("slab", None, "row", None),
            P("slab", None, None, None, "row"),
            P("slab", None),
        ),
        out_specs=P("slab", None, None, None, "row"),
        check_vma=False,
    )
```

time: 905 us -> 293 us (0.32); the launches traced: 895 us -> 293 us
  local copies, waits for them, and re-layouts: 443 us -> 6.85 us
  Pallas kernels: 0 us -> 286 us
  waiting for transfers between devices: 233 us -> 0 us
  other arithmetic: 118 us -> 0 us
  matrix products: 84.1 us -> 0 us
  between operations: 13.3 us -> 0.01 us
    pallas_call x0 -> x1, Pallas kernels: none -> 286 us  [on_device(): pl.pallas_call(functools.partial(kernel, slabs, count), out_shape=jax.Sha...]
    all_gather x4 -> x0, waiting for transfers between devices: 212 us -> none  [on_device(): lax.all_gather(incoming, 'row', axis=3, tiled=True)]
    gather x1 -> x0, local copies, waits for them, and re-layouts: 194 us -> none  [permute_columns(): return jnp.take(matrix, inverse, axis=2)]
    unnamed x20 -> x0, local copies, waits for them, and re-layouts: 122 us -> none
    select_n x7 -> x0, other arithmetic: 105 us -> none  [the longest x2 100 us: permute_columns(): return jnp.take(matrix, inverse, axis=2)]
    dot_general x4 -> x0, matrix products: 84.1 us -> none  [complex_apply(): lax.dot_general(flat, mflat, (((1,), (1,)), ((), ())), preferred_element_...]
    select_n x2 -> x0, local copies, waits for them, and re-layouts: 81.9 us -> none  [the longest x1 81 us: permute_columns(): return jnp.take(matrix, inverse, axis=2)]
    scatter x1 -> x0, local copies, waits for them, and re-layouts: 30.5 us -> none  [permute_columns(): jnp.zeros((total_cols,), jnp.int32).at[order]]
  transfers between devices with their start and end apart: 7 -> 0, of which waited for: 5 -> 0; matrix products, arithmetic and copies ran while one was open for 57% -> 0% of each run, Pallas kernels for 0% -> 0%
where the time goes in v1:
time: 293 us
  Pallas kernels  286 us (98%)
  local copies, waits for them, and re-layouts  6.85 us (2%)
    pallas_call x1, Pallas kernels, on_device(): pl.pallas_call(functools.partial(kernel, slabs, count), out_shape=jax.Sha...  286 us

profile of v1, /device:TPU:3, one launch (start us, length us, event | category | flops | bytes accessed | tf_op | source)
XLA Modules:
  0.0 293.1 jit_solution(18192388805536610140)
XLA Ops:
  0.0 2.3 copy.8
  2.3 2.3 copy.9
  4.6 286.2 %shard_map.46 = bf16[3,1024,128]{2,1,0:T(8,128)(2,1)} custom-call(s32[8192]{0:T(1024)} %bitcast.14, bf16[3,1024,128]{2,1,0:T(8,128)(2,1)} %bitcast.10, bf16[2048,8192]{1,0:T(8,128)(2,1)} %bitcast.8, bf16[3,1024,128]{2,1,0:T(8,128)(2,1)} %bitcast.11), custom_call_target="tpu_custom_call" | custom-call | tf_op jit(solution)/shard_map/pallas_call | solution.py:183
  290.8 2.3 copy.10

commit v2 on v1

v2 whole, which is shorter than its diff:
```python
import functools

import jax
import jax.numpy as jnp
from jax import lax
from jax.experimental import pallas as pl
from jax.experimental.pallas import tpu as pltpu
from jax.sharding import PartitionSpec as P

MESH = pl.DeviceIdType.MESH


def ring_to_row(position, count):
    return jnp.where(position < count // 2, 2 * position, 2 * (count - 1 - position) + 1)


def row_to_ring(row, count):
    return jnp.where(row % 2 == 0, row // 2, count - 1 - row // 2)


MARKS = (1, 2, 4, 5, 6)


def kernel(
    slabs, count, pieces,
    skel, rhs, op, src, out,
    matrix, recv, xf, xb,
    msem, lsem, right_send, right_recv, left_send, left_recv, pass_send, pass_recv,
):
    batches = rhs.shape[0]
    rows = rhs.shape[1]
    width = rhs.shape[2]
    depth = rows * count
    half = width // 2
    size = rows // pieces
    slab = lax.axis_index("slab")
    row = lax.axis_index("row")
    place = row_to_ring(row, count)
    right = ring_to_row((place + 1) % count, count)
    left = ring_to_row((place + count - 1) % count, count)
    first = slab == 0
    inner = slab < slabs - 1
    right_steps = count // 2
    left_steps = count - 1 - right_steps

    def load(piece, part):
        return pltpu.make_async_copy(
            op.at[part, pl.ds(piece * size, size)],
            matrix.at[pl.ds((2 * piece + part) * size, size)],
            msem.at[piece, part],
        )

    barrier = pltpu.get_barrier_semaphore()
    pl.semaphore_signal(barrier, inc=1, device_id={"slab": slab, "row": right}, device_id_type=MESH)
    pl.semaphore_signal(barrier, inc=1, device_id={"slab": slab, "row": left}, device_id_type=MESH)

    @pl.when(inner)
    def _():
        pl.semaphore_signal(barrier, inc=1, device_id={"slab": slab + 1, "row": row}, device_id_type=MESH)

    @pl.when(jnp.logical_not(first))
    def _():
        pl.semaphore_signal(barrier, inc=1, device_id={"slab": slab - 1, "row": row}, device_id_type=MESH)

    def own(batch):
        return pltpu.make_async_copy(
            rhs.at[batch], recv.at[batch, pl.ds(pl.multiple_of(row * rows, rows), rows)], lsem.at[batch]
        )

    @pl.when(first)
    def _():
        for batch in range(batches):
            own(batch).start()

    for piece in range(pieces):
        for part in range(2):
            load(piece, part).start()

    @pl.when(first)
    def _():
        for batch in range(batches):
            own(batch).wait()

    pl.semaphore_wait(barrier, 2 + jnp.where(inner, 1, 0) + jnp.where(first, 0, 1))

    def held(batch, owner, piece):
        return recv.at[batch, pl.ds(pl.multiple_of(owner * rows + piece * size, size), size)]

    def rightward(batch, piece, step):
        data = held(batch, ring_to_row((place + count - step) % count, count), piece)
        return pltpu.make_async_remote_copy(
            src_ref=data, dst_ref=data,
            send_sem=right_send.at[batch, piece, step], recv_sem=right_recv.at[batch, piece, step],
            device_id={"slab": slab, "row": right}, device_id_type=MESH,
        )

    def leftward(batch, piece, step):
        data = held(batch, ring_to_row((place + step) % count, count), piece)
        return pltpu.make_async_remote_copy(
            src_ref=data, dst_ref=data,
            send_sem=left_send.at[batch, piece, step], recv_sem=left_recv.at[batch, piece, step],
            device_id={"slab": slab, "row": left}, device_id_type=MESH,
        )

    def passing(batch, piece):
        return pltpu.make_async_remote_copy(
            src_ref=out.at[batch, pl.ds(piece * size, size)], dst_ref=held(batch, row, piece),
            send_sem=pass_send.at[batch, piece], recv_sem=pass_recv.at[batch, piece],
            device_id={"slab": jnp.minimum(slab + 1, slabs - 1), "row": row}, device_id_type=MESH,
        )

    def splits(piece):
        if count % 2 or pieces == 1:
            return right_steps, left_steps
        if piece < pieces // 2:
            return count // 2, count // 2 - 1
        return count // 2 - 1, count // 2

    def advance(batch, piece, step):
        rights, lefts = splits(piece)
        if step == 0:
            @pl.when(jnp.logical_not(first))
            def _():
                passing(batch, piece).wait_recv()
        else:
            if step <= rights:
                rightward(batch, piece, step - 1).wait_recv()
            if step <= lefts:
                leftward(batch, piece, step - 1).wait_recv()
        if step < rights:
            rightward(batch, piece, step).start()
        if step < lefts:
            leftward(batch, piece, step).start()

    steps = right_steps + 1
    waves = steps + pieces - 1

    def wave(batch, now):
        for piece in range(pieces):
            if 0 <= now - piece < steps:
                advance(batch, piece, now - piece)

    def waves_of_next(batch, low, high):
        if low < high:
            @pl.when(batch + 1 < batches)
            def _():
                for now in range(low, high):
                    wave(batch + 1, now)

    for now in range(waves):
        wave(0, now)

    spread = 8
    group = 128
    marks = [min(waves, mark) for mark in MARKS]

    def gather(start, stop):
        @pl.loop(start, stop)
        def _(chunk):
            base = pl.multiple_of(chunk * group, group)
            for lump in range(group // 16):
                picked = [xf[pl.ds(skel[base + lump * 16 + offset], 1), :] for offset in range(16)]
                xb[pl.ds(pl.multiple_of(base + lump * 16, 16), 16), :] = jnp.concatenate(picked, axis=0).astype(jnp.bfloat16)

    @pl.loop(0, batches)
    def _(batch):
        span = depth // spread

        @pl.loop(0, spread)
        def _(part):
            at = pl.ds(pl.multiple_of(part * span, span), span)
            xf[at, :] = recv[batch, at, :].astype(jnp.float32)

        chunks = depth // group
        gather(0, chunks // 2)
        waves_of_next(batch, 0, marks[0])
        gather(chunks // 2, chunks)
        waves_of_next(batch, marks[0], marks[1])

        for piece in range(pieces):
            @pl.when(batch == 0)
            def _():
                for part in range(2):
                    load(piece, part).wait()

            joined = jnp.dot(
                matrix[pl.ds(2 * piece * size, 2 * size), :], xb[...], preferred_element_type=jnp.float32
            )
            lane = lax.broadcasted_iota(jnp.int32, (size, width), 1)
            turned = pltpu.roll(joined[size:], half, axis=1)
            total = joined[:size] + jnp.where(lane < half, -turned, turned)
            at = pl.ds(piece * size, size)
            out[batch, at, :] = (total + src[batch, at, :].astype(jnp.float32)).astype(jnp.bfloat16)

            @pl.when(inner)
            def _():
                passing(batch, piece).start()

            low = marks[min(len(marks) - 1, piece + 1)]
            high = waves if piece == pieces - 1 else marks[min(len(marks) - 1, piece + 2)]
            waves_of_next(batch, low, high)

    @pl.loop(0, batches)
    def _(batch):
        for piece in range(pieces):
            rights, lefts = splits(piece)
            for step in range(rights):
                rightward(batch, piece, step).wait_send()
            for step in range(lefts):
                leftward(batch, piece, step).wait_send()

            @pl.when(inner)
            def _():
                passing(batch, piece).wait_send()


def on_device(rhs, operator, sources, skeleton):
    slabs = lax.axis_size("slab")
    count = lax.axis_size("row")
    batches, two, lanes, rows = rhs.shape
    depth = operator.shape[3]
    width = two * lanes
    flipped = rhs.reshape(batches, width, rows).transpose(0, 2, 1)
    added = sources[0].reshape(batches, width, rows).transpose(0, 2, 1)
    half = max(1, count // 2)
    pieces = 4 if count <= 8 else 1
    result = pl.pallas_call(
        functools.partial(kernel, slabs, count, pieces),
        out_shape=jax.ShapeDtypeStruct((batches, rows, width), jnp.bfloat16),
        in_specs=[
            pl.BlockSpec(memory_space=pltpu.SMEM),
            pl.BlockSpec(memory_space=pltpu.VMEM),
            pl.BlockSpec(memory_space=pl.ANY),
            pl.BlockSpec(memory_space=pltpu.VMEM),
        ],
        out_specs=pl.BlockSpec(memory_space=pltpu.VMEM),
        scratch_shapes=[
            pltpu.VMEM((2 * rows, depth), jnp.bfloat16),
            pltpu.VMEM((batches, depth, width), jnp.bfloat16),
            pltpu.VMEM((depth, width), jnp.float32),
            pltpu.VMEM((depth, width), jnp.bfloat16),
            pltpu.SemaphoreType.DMA((pieces, 2)),
            pltpu.SemaphoreType.DMA((batches,)),
            pltpu.SemaphoreType.DMA((batches, pieces, half)),
            pltpu.SemaphoreType.DMA((batches, pieces, half)),
            pltpu.SemaphoreType.DMA((batches, pieces, half)),
            pltpu.SemaphoreType.DMA((batches, pieces, half)),
            pltpu.SemaphoreType.DMA((batches, pieces)),
            pltpu.SemaphoreType.DMA((batches, pieces)),
        ],
        compiler_params=pltpu.CompilerParams(
            collective_id=0, has_side_effects=True, vmem_limit_bytes=60 * 1024 * 1024
        ),
    )(skeleton[0], flipped, operator[0], added)
    return result.transpose(0, 2, 1).reshape(batches, two, lanes, rows)[None]


def solution(mesh):
    return jax.shard_map(
        on_device,
        mesh=mesh,
        in_specs=(
            P(None, None, None, "row"),
            P("slab", None, "row", None),
            P("slab", None, None, None, "row"),
            P("slab", None),
        ),
        out_specs=P("slab", None, None, None, "row"),
        check_vma=False,
    )
```

time: 293 us -> 284 us (0.969)
  Pallas kernels: 286 us -> 277 us
    pallas_call x1, Pallas kernels: 286 us -> 277 us  [on_device(): pl.pallas_call(functools.partial(kernel, slabs, count, pieces), out_shape...]
where the time goes in v2:
time: 284 us
  Pallas kernels  277 us (98%)
  local copies, waits for them, and re-layouts  6.85 us (2%)
    pallas_call x1, Pallas kernels, on_device(): pl.pallas_call(functools.partial(kernel, slabs, count, pieces), out_shape...  277 us

profile of v2, /device:TPU:3, one launch (start us, length us, event | category | flops | bytes accessed | tf_op | source)
XLA Modules:
  0.0 284.2 jit_solution(11554274849621905811)
XLA Ops:
  0.0 2.3 copy.8
  2.3 2.3 copy.9
  4.6 277.3 %shard_map.46 = bf16[3,1024,128]{2,1,0:T(8,128)(2,1)} custom-call(s32[8192]{0:T(1024)} %bitcast.14, bf16[3,1024,128]{2,1,0:T(8,128)(2,1)} %bitcast.10, bf16[2,1024,8192]{2,1,0:T(8,128)(2,1)} %bitcast.8, bf16[3,1024,128]{2,1,0:T(8,128)(2,1)} %bitcast.11), custom_call_target="tpu_custom_call" | custom-call | tf_op jit(solution)/shard_map/pallas_call | solution.py:227
  281.9 2.3 copy.10

commit v3 on v2

--- a/solution.py
+++ b/solution.py
@@ -18,7 +18,7 @@
     return jnp.where(row % 2 == 0, row // 2, count - 1 - row // 2)
 
 
-MARKS = (1, 2, 4, 5, 6)
+MARKS = (1, 2, 3, 4, 5, 6, 7)
 
 
 def kernel(
@@ -165,6 +165,7 @@
     @pl.loop(0, batches)
     def _(batch):
         span = depth // spread
+        waves_of_next(batch, 0, marks[0])
 
         @pl.loop(0, spread)
         def _(part):
@@ -172,10 +173,9 @@
             xf[at, :] = recv[batch, at, :].astype(jnp.float32)
 
         chunks = depth // group
-        gather(0, chunks // 2)
-        waves_of_next(batch, 0, marks[0])
-        gather(chunks // 2, chunks)
-        waves_of_next(batch, marks[0], marks[1])
+        for part in range(4):
+            gather(part * chunks // 4, (part + 1) * chunks // 4)
+            waves_of_next(batch, marks[part], marks[part + 1])
 
         for piece in range(pieces):
             @pl.when(batch == 0)
@@ -196,8 +196,8 @@
             def _():
                 passing(batch, piece).start()
 
-            low = marks[min(len(marks) - 1, piece + 1)]
-            high = waves if piece == pieces - 1 else marks[min(len(marks) - 1, piece + 2)]
+            low = marks[min(len(marks) - 1, piece + 4)]
+            high = waves if piece == pieces - 1 else marks[min(len(marks) - 1, piece + 5)]
             waves_of_next(batch, low, high)
 
     @pl.loop(0, batches)

time: 284 us -> 299 us (1.053)
  Pallas kernels: 277 us -> 292 us
    pallas_call x1, Pallas kernels: 277 us -> 292 us  [on_device(): pl.pallas_call(functools.partial(kernel, slabs, count, pieces), out_shape...]
where the time goes in v3:
time: 299 us; the launch traced here: 298 us
  Pallas kernels  292 us (98%)
  local copies, waits for them, and re-layouts  6.85 us (2%)
    pallas_call x1, Pallas kernels, on_device(): pl.pallas_call(functools.partial(kernel, slabs, count, pieces), out_shape...  292 us

profile of v3, /device:TPU:3, one launch (start us, length us, event | category | flops | bytes accessed | tf_op | source)
XLA Modules:
  0.0 298.5 jit_solution(5122649007940030614)
XLA Ops:
  0.0 2.3 copy.8
  2.3 2.3 copy.9
  4.6 291.6 %shard_map.46 = bf16[3,1024,128]{2,1,0:T(8,128)(2,1)} custom-call(s32[8192]{0:T(1024)} %bitcast.14, bf16[3,1024,128]{2,1,0:T(8,128)(2,1)} %bitcast.10, bf16[2,1024,8192]{2,1,0:T(8,128)(2,1)} %bitcast.8, bf16[3,1024,128]{2,1,0:T(8,128)(2,1)} %bitcast.11), custom_call_target="tpu_custom_call" | custom-call | tf_op jit(solution)/shard_map/pallas_call | solution.py:227
  296.2 2.3 copy.10
